TPU v7x, 32 devices: a whole 2x2x4 slice. The times are simulated.
32 devices in a mesh: chan: 4 (over y, x), space: 4 (over z), rep: 2 (over core).
Axes of the slice: x: 2, y: 2, z: 4, core: 2. Of those that a mesh axis runs over, the one named last changes fastest.
Arguments:
- inputs: bfloat16 [2, 2, 16, 512, 128], P('rep', None, 'space', 'chan'), may hold values from -6 to 6
- grad_out: bfloat16 [2, 2, 16, 512, 128], P('rep', None, 'space', 'chan'), may hold values from -6 to 6
- weight: bfloat16 [3, 3, 3, 512, 512], P(None, None, None, 'chan'), may hold values from -0.0546875 to 0.0546875
Outputs:
- grad_in: bfloat16 [2, 2, 16, 512, 128], P('rep', None, 'space', 'chan')
- grad_weight: float32 [3, 3, 3, 512, 512], P(None, None, None, ('chan', 'rep'))
All inputs are finite; a program needn't handle non-finite values.
Results may differ from a plain program's by a relative error of at most 0.0031.
Values may be sent and summed in bfloat16 or wider, within the bound.
A program may use at most 64 MiB of HBM per device.

v0:
```python
import jax
import jax.numpy as jnp
from jax import lax
from jax.sharding import PartitionSpec as P


def with_halo(cells, sides, width):
    for axis, dim in sides:
        count = lax.axis_size(axis)
        ends = count - 1
        head = lax.slice_in_dim(cells, 0, width, axis=dim)
        tail = lax.slice_in_dim(cells, cells.shape[dim] - width, cells.shape[dim], axis=dim)
        cells = jnp.concatenate(
            [
                lax.ppermute(tail, axis, [(i, (i + 1) % count) for i in range(ends)]),
                cells,
                lax.ppermute(head, axis, [((i + 1) % count, i) for i in range(ends)]),
            ],
            axis=dim,
        )
    return cells


def silu_slope(values):
    logistic = jax.nn.sigmoid(values)
    return logistic * (1.0 + values * (1.0 - logistic))


def tap_windows(padded, frame_count, row_count, col_count):
    windows = []
    for frame_tap in range(3):
        for row_tap in range(3):
            for col_tap in range(3):
                windows.append(
                    padded[
                        :,
                        2 - frame_tap : 2 - frame_tap + frame_count,
                        2 - row_tap : 2 - row_tap + row_count,
                        :,
                        2 - col_tap : 2 - col_tap + col_count,
                    ]
                )
    return jnp.concatenate(windows, axis=3)


def on_device(inputs, grad_out, weight):
    clip_count, frame_count, row_count, in_part, col_count = inputs.shape
    out_part = grad_out.shape[3]
    gathered = lax.all_gather(inputs, "chan", axis=3, tiled=True)
    activated = jax.nn.silu(gathered.astype(jnp.float32)).astype(jnp.bfloat16)
    in_width = activated.shape[3]
    grad_rim = with_halo(grad_out, (("space", 2),), 1)
    grad_pad = jnp.pad(grad_rim, ((0, 0), (0, 2), (0, 0), (0, 0), (1, 1)))
    stacked = tap_windows(grad_pad, frame_count, row_count, col_count)
    local_flat = jnp.einsum(
        "cthkw,cthiw->ki", stacked, activated, preferred_element_type=jnp.float32
    )
    local_weight = local_flat.reshape(3, 3, 3, out_part, in_width)
    clip_summed = lax.psum_scatter(local_weight, "rep", scatter_dimension=3, tiled=True)
    summed = lax.psum(clip_summed, "space")
    grad_weight = summed * (1.0 / 256.0)
    flat_kernel = weight.reshape(27 * out_part, weight.shape[4])
    partial_value = jnp.einsum(
        "cthkw,ki->cthiw", stacked, flat_kernel, preferred_element_type=jnp.float32
    )
    active_grad = lax.psum_scatter(partial_value, "chan", scatter_dimension=3, tiled=True)
    grad_in = (active_grad * silu_slope(inputs.astype(jnp.float32))).astype(jnp.bfloat16)
    return (grad_in, grad_weight)


def solution(mesh):
    return jax.shard_map(
        on_device,
        mesh=mesh,
        in_specs=(
            P("rep", None, "space", "chan", None),
            P("rep", None, "space", "chan", None),
            P(None, None, None, "chan", None),
        ),
        out_specs=(
            P("rep", None, "space", "chan", None),
            P(None, None, None, ("chan", "rep"), None),
        ),
        check_vma=False,
    )
```

profile of v0, /device:TPU:0, one launch (start us, length us, event | category | flops | bytes accessed | tf_op | source)
XLA Modules:
  0.0 258.9 jit_solution(6788880601391279087)
XLA Ops:
  7.2 1.9 copy.15
  9.2 1.5 fusion.32
  10.7 1.3 collective-permute-start.1
  12.0 6.2 %collective-permute-start = (bf16[1,2,1,128,128]{3,4,2,1,0:T(8,128)(2,1)}, bf16[1,2,1,128,128]{3,4,2,1,0:T(8,128)(2,1)}, u32[]{:S(2)}, u32[]{:S(2)}) collective-permute-start(bf16[1,2,1,128,128]{3,4,2,1,0:T(8,128)(2,1)} %get-tuple-element.6), channel_id=1, source_target_pairs={{0,2},{2,4},{4,6},{1,3},{3,5},{5,7},{8,10},{10,12},{12,14},{9,11},... | collective-permute-start | bytes 196616 | tf_op jit(solution)/shard_map/ppermute | solution.py:15
  19.1 0.6 collective-permute-done
  19.7 1.2 fusion.20
  20.9 0.1 slice_dynamic-update-slice_fusion.14
  21.3 0.1 slice_dynamic-update-slice_fusion.10
  21.6 0.1 slice_dynamic-update-slice_fusion.8
  22.0 0.9 fusion.31
  23.4 0.9 fusion.30
  24.4 2.9 %copy-done.2 = bf16[1,2,4,3456,128]{3,4,2,1,0:T(8,128)(2,1)} copy-done((bf16[1,2,4,3456,128]{3,4,2,1,0:T(8,128)(2,1)}, bf16[1,2,4,3456,128]{3,4,2,1,0:T(8,128)(2,1)S(1)}, u32[]{:S(2)}) %copy-start.2) | copy-done | bytes 7077912
  27.3 10.2 %copy.22 = bf16[3456,4,2,128]{3,0,2,1:T(8,128)(2,1)} copy(bf16[3456,4,2,128]{0,3,1,2:T(8,128)(2,1)} %bitcast.31) | data formatting | bytes 14155776 | tf_op jit(solution)/shard_map/cthkw,cthiw->ki/dot_general | solution.py:55
  37.5 8.1 %all-gather.2.cloned.1.call-done = bf16[1,2,4,512,128]{4,3,2,1,0:T(8,128)(2,1)} async-done(((bf16[1,2,4,128,128]{4,3,2,1,0:T(8,128)(2,1)}), bf16[1,2,4,512,128]{4,3,2,1,0:T(8,128)(2,1)}) %all-gather.2.cloned.1.call-update) | async-done | bytes 1048592 | tf_op jit(solution)/shard_map/all_gather | solution.py:49
  45.6 6.6 %fusion = f32[3,3,3,128,512,1,1]{4,3,0,1,2,6,5:T(8,128)S(1)} fusion(bf16[3,3,3,128,4,2,128]{6,3,2,1,0,5,4:T(8,128)(2,1)} %bitcast.32, bf16[1,2,4,512,128]{4,3,2,1,0:T(8,128)(2,1)} %all-gather.2.cloned.1.call-done), kind=kOutput, calls=%fused_computation | convolution fusion | flops 3627024384 | bytes 15204352 | tf_op jit(solution)/shard_map/cthkw,cthiw->ki/dot_general | solution.py:55
  52.3 3.7 %copy.38 = f32[3,3,3,128,512,1,1]{4,3,2,1,0,5,6:T(8,128)} copy(f32[3,3,3,128,512,1,1]{4,3,0,1,2,6,5:T(8,128)S(1)} %fusion) | data formatting | bytes 14155776 | tf_op jit(solution)/shard_map/cthkw,cthiw->ki/dot_general | solution.py:55
  56.1 7.5 %fusion.13 = f32[1,2,4,512,128]{3,4,2,1,0:T(8,128)} fusion(bf16[3456,512,1,1]{1,0,3,2:T(8,128)(2,1)S(1)} %bitcast.29, bf16[1,2,4,3456,128]{3,4,2,1,0:T(8,128)(2,1)} %copy-done.2), kind=kOutput, calls=%fused_computation.20 | convolution fusion | flops 3623878656 | bytes 12713984 | tf_op jit(solution)/shard_map/cthkw,ki->cthiw/dot_general | solution.py:63
  63.7 7.9 %reduce-scatter.5.cloned.1.call-done = f32[3,3,3,64,512]{4,3,2,1,0:T(8,128)} async-done(((f32[3,3,3,128,512]{4,3,2,1,0:T(8,128)}), f32[3,3,3,64,512]{4,3,2,1,0:T(8,128)}) %reduce-scatter.5.cloned.1.call-update) | async-done | bytes 3538960 | tf_op jit(solution)/shard_map/reduce_scatter | solution.py:59
  71.7 1.8 copy.21
  73.5 38.5 %reduce-scatter.3.cloned.1.call-done = f32[1,2,4,128,128]{3,4,2,1,0:T(8,128)} async-done(((f32[1,2,4,512,128]{3,4,2,1,0:T(8,128)}), f32[1,2,4,128,128]{3,4,2,1,0:T(8,128)}) %reduce-scatter.3.cloned.1.call-update) | async-done | bytes 524304 | tf_op jit(solution)/shard_map/reduce_scatter | solution.py:66
  111.9 2.0 fusion.29
  113.9 1.8 copy.25
  115.7 132.2 %all-reduce.3.cloned.1.call-done = f32[3,3,3,64,512]{4,3,2,1,0:T(8,128)} async-done(((f32[3,3,3,64,512]{4,3,2,1,0:T(8,128)}), f32[3,3,3,64,512]{4,3,2,1,0:T(8,128)}) %all-reduce.3.cloned.1.call-update) | async-done | bytes 3538960 | tf_op jit(solution)/shard_map/psum | solution.py:60
  248.0 4.4 %broadcast_multiply_fusion = f32[3,3,3,64,512]{4,3,2,1,0:T(8,128)} fusion(f32[3,3,3,64,512]{4,3,2,1,0:T(8,128)} %all-reduce.3.cloned.1.call-done), kind=kLoop, calls=%fused_computation.13 | loop fusion | flops 884736 | bytes 7077888 | tf_op jit(solution)/shard_map/mul | solution.py:61
  (36 shorter events, 2.2 us)
Async XLA Ops:
  7.2 48.9 %copy-start = (bf16[3,3,3,128,512]{4,3,2,1,0:T(8,128)(2,1)S(1)}, bf16[3,3,3,128,512]{4,3,2,1,0:T(8,128)(2,1)}, u32[]{:S(2)}) copy-start(bf16[3,3,3,128,512]{4,3,2,1,0:T(8,128)(2,1)} %param.5) | copy-start | bytes 10616836
  7.2 38.5 %all-gather.2.cloned.1.call-start = ((), (), s32[]{:S(2)}) async-start(), calls=%async_computation.3 | async-start | bytes 1310720 | tf_op jit(solution)/shard_map/all_gather | solution.py:49
  10.7 8.5 %collective-permute-start.1 = (bf16[1,2,1,128,128]{3,4,2,1,0:T(8,128)(2,1)}, bf16[1,2,1,128,128]{3,4,2,1,0:T(8,128)(2,1)}, u32[]{:S(2)}, u32[]{:S(2)}) collective-permute-start(bf16[1,2,1,128,128]{3,4,2,1,0:T(8,128)(2,1)} %get-tuple-element.7), channel_id=1, source_target_pairs={{2,0},{4,2},{6,4},{3,1},{5,3},{7,5},{10,8},{12,10},{14,12},{11,9},... | collective-permute-start | bytes 196616 | tf_op jit(solution)/shard_map/ppermute | solution.py:17
  12.0 7.8 %collective-permute-start = (bf16[1,2,1,128,128]{3,4,2,1,0:T(8,128)(2,1)}, bf16[1,2,1,128,128]{3,4,2,1,0:T(8,128)(2,1)}, u32[]{:S(2)}, u32[]{:S(2)}) collective-permute-start(bf16[1,2,1,128,128]{3,4,2,1,0:T(8,128)(2,1)} %get-tuple-element.6), channel_id=1, source_target_pairs={{0,2},{2,4},{4,6},{1,3},{3,5},{5,7},{8,10},{10,12},{12,14},{9,11},... | collective-permute-start | bytes 196616 | tf_op jit(solution)/shard_map/ppermute | solution.py:15
  18.2 53.4 %reduce-scatter.5.cloned.1.call-start = ((), (), s32[]{:S(2)}) async-start(), calls=%async_computation.4 | async-start | bytes 10616832 | tf_op jit(solution)/shard_map/reduce_scatter | solution.py:59
  18.2 3.8 %copy-start.1 = (bf16[1,2,4,128,128]{3,4,2,1,0:T(8,128)(2,1)S(1)}, bf16[1,2,4,128,128]{3,4,2,1,0:T(8,128)(2,1)}, u32[]{:S(2)}) copy-start(bf16[1,2,4,128,128]{3,4,2,1,0:T(8,128)(2,1)} %copy.15) | copy-start | bytes 786436
  24.4 2.9 %copy-start.2 = (bf16[1,2,4,3456,128]{3,4,2,1,0:T(8,128)(2,1)}, bf16[1,2,4,3456,128]{3,4,2,1,0:T(8,128)(2,1)S(1)}, u32[]{:S(2)}) copy-start(bf16[1,2,4,3456,128]{3,4,2,1,0:T(8,128)(2,1)S(1)} %slice_dynamic-update-slice_fusion) | copy-start | bytes 21233668
  56.0 55.9 %reduce-scatter.3.cloned.1.call-start = ((), (), s32[]{:S(2)}) async-start(), calls=%async_computation.2 | async-start | bytes 2621440 | tf_op jit(solution)/shard_map/reduce_scatter | solution.py:66
  63.7 184.3 %all-reduce.3.cloned.1.call-start = ((), (), s32[]{:S(2)}) async-start(), calls=%async_computation.5 | async-start | bytes 7077888 | tf_op jit(solution)/shard_map/psum | solution.py:60
Sparse Core Ops, SparseCore 0:
  18.3 27.2 all-gather.1
  56.2 15.4 reduce-scatter.4
  75.5 36.4 reduce-scatter.2
  114.2 133.7 all-reduce.2
where the time goes:
time: 260 us; the launch traced here: 259 us
  waiting for transfers between devices  187 us (72%)
  local copies, waits for them, and re-layouts  26.3 us (10%)
  matrix products  14.2 us (5%)
  between operations  14 us (5%)
  other arithmetic  9.39 us (4%)
  starting transfers between devices  7.63 us (3%)
    psum x1, waiting for transfers between devices, on_device(): summed = lax.psum(clip_summed, 'space')  132 us
    reduce_scatter x1, waiting for transfers between devices, on_device(): lax.psum_scatter(partial_value, 'chan', scatter_dimension=3, tiled=True)  38.5 us
    dot_general x2, local copies, waits for them, and re-layouts, on_device(): jnp.einsum('cthkw,cthiw->ki', stacked, activated, preferred_element_type=...  14 us
    unnamed x33, local copies, waits for them, and re-layouts  10.7 us
    all_gather x1, waiting for transfers between devices, on_device(): gathered = lax.all_gather(inputs, 'chan', axis=3, tiled=True)  8.09 us
    reduce_scatter x1, waiting for transfers between devices, on_device(): lax.psum_scatter(local_weight, 'rep', scatter_dimension=3, tiled=True)  7.92 us
    dot_general x1, matrix products, on_device(): jnp.einsum('cthkw,ki->cthiw', stacked, flat_kernel, preferred_element_typ...  7.54 us
    dot_general x1, matrix products, on_device(): jnp.einsum('cthkw,cthiw->ki', stacked, activated, preferred_element_type=...  6.64 us
  transfers between devices with their start and end apart: 6, of which 5 were waited for; matrix products, arithmetic and copies ran while one was open for 11% of the time, Pallas kernels for 0%

commit v1 on v0

--- a/solution.py
+++ b/solution.py
@@ -57,7 +57,7 @@
     )
     local_weight = local_flat.reshape(3, 3, 3, out_part, in_width)
     clip_summed = lax.psum_scatter(local_weight, "rep", scatter_dimension=3, tiled=True)
-    summed = lax.psum(clip_summed, "space")
+    summed = jnp.sum(lax.all_gather(clip_summed, "space"), axis=0)
     grad_weight = summed * (1.0 / 256.0)
     flat_kernel = weight.reshape(27 * out_part, weight.shape[4])
     partial_value = jnp.einsum(

time: 260 us -> 371 us (1.43)
  waiting for transfers between devices: 187 us -> 289 us
  other arithmetic: 9.39 us -> 16.7 us
    all_gather x0 -> x1, waiting for transfers between devices: none -> 242 us  [on_device(): summed = jnp.sum(lax.all_gather(clip_summed, 'space'), axis=0)]
    psum x1 -> x0, waiting for transfers between devices: 132 us -> none  [on_device(): summed = lax.psum(clip_summed, 'space')]
    reduce_sum x0 -> x1, other arithmetic: none -> 9 us  [on_device(): summed = jnp.sum(lax.all_gather(clip_summed, 'space'), axis=0)]
    all_gather x1, waiting for transfers between devices: 8.09 us -> 1.25 us  [on_device(): gathered = lax.all_gather(inputs, 'chan', axis=3, tiled=True)]
    reduce_scatter x1, waiting for transfers between devices: 38.5 us -> 33.5 us  [on_device(): lax.psum_scatter(partial_value, 'chan', scatter_dimension=3, tiled=True)]
    reduce_scatter x0 -> x1, local copies, waits for them, and re-layouts: none -> 4.39 us  [on_device(): lax.psum_scatter(local_weight, 'rep', scatter_dimension=3, tiled=True)]
    ppermute x1, waiting for transfers between devices: 0.01 us -> 3.97 us  [with_halo(): lax.ppermute(head, axis, [((i + 1) % count, i) for i in range(ends)])]
  transfers between devices with their start and end apart: 6 -> 6, of which waited for: 5 -> 5; matrix products, arithmetic and copies ran while one was open for 11% -> 9% of each run, Pallas kernels for 0% -> 0%
where the time goes in v1:
time: 371 us
  waiting for transfers between devices  289 us (78%)
  local copies, waits for them, and re-layouts  30 us (8%)
  other arithmetic  16.7 us (5%)
  matrix products  14.2 us (4%)
  between operations  14 us (4%)
  starting transfers between devices  6.38 us (2%)
    all_gather x1, waiting for transfers between devices, on_device(): summed = jnp.sum(lax.all_gather(clip_summed, 'space'), axis=0)  242 us
    reduce_scatter x1, waiting for transfers between devices, on_device(): lax.psum_scatter(partial_value, 'chan', scatter_dimension=3, tiled=True)  33.5 us
    dot_general x2, local copies, waits for them, and re-layouts, on_device(): jnp.einsum('cthkw,cthiw->ki', stacked, activated, preferred_element_type=...  13.8 us
    unnamed x33, local copies, waits for them, and re-layouts  10.9 us
    reduce_sum x1, other arithmetic, on_device(): summed = jnp.sum(lax.all_gather(clip_summed, 'space'), axis=0)  9 us
    reduce_scatter x1, waiting for transfers between devices, on_device(): lax.psum_scatter(local_weight, 'rep', scatter_dimension=3, tiled=True)  7.9 us
    dot_general x1, matrix products, on_device(): jnp.einsum('cthkw,ki->cthiw', stacked, flat_kernel, preferred_element_typ...  7.57 us
  transfers between devices with their start and end apart: 6, of which 5 were waited for; matrix products, arithmetic and copies ran while one was open for 9% of the time, Pallas kernels for 0%

profile of v1, /device:TPU:0, one launch (start us, length us, event | category | flops | bytes accessed | tf_op | source)
XLA Modules:
  0.0 370.8 jit_solution(9080213999918443456)
XLA Ops:
  7.2 0.7 all-gather.4.cloned.1.call-update
  8.0 2.1 copy.26
  10.0 0.9 fusion.31
  11.0 4.9 %collective-permute-start = (bf16[1,2,1,128,128]{3,4,2,1,0:T(8,128)(2,1)S(1)}, bf16[1,2,1,128,128]{3,4,2,1,0:T(8,128)(2,1)S(1)}, u32[]{:S(2)}, u32[]{:S(2)}) collective-permute-start(bf16[1,2,1,128,128]{3,4,2,1,0:T(8,128)(2,1)S(1)} %get-tuple-element.8), channel_id=1, source_target_pairs={{0,2},{2,4},{4,6},{1,3},{3,5},{5,7},{8,10},{10,12},{12,14},{9,11},... | collective-permute-start | bytes 196616 | tf_op jit(solution)/shard_map/ppermute | solution.py:15
  15.9 1.3 collective-permute-start.1
  18.1 4.0 %collective-permute-done.1 = bf16[1,2,1,128,128]{3,4,2,1,0:T(8,128)(2,1)S(1)} collective-permute-done((bf16[1,2,1,128,128]{3,4,2,1,0:T(8,128)(2,1)S(1)}, bf16[1,2,1,128,128]{3,4,2,1,0:T(8,128)(2,1)S(1)}, u32[]{:S(2)}, u32[]{:S(2)}) %collective-permute-start.1) | collective-permute-done | bytes 65568 | tf_op jit(solution)/shard_map/ppermute | solution.py:17
  22.1 1.1 fusion.19
  23.8 0.1 slice_dynamic-update-slice_fusion.8
  24.0 0.1 slice_dynamic-update-slice_fusion.7
  25.0 2.9 copy-done.2
  27.9 10.1 %copy.33 = bf16[3456,4,2,128]{3,0,2,1:T(8,128)(2,1)} copy(bf16[3456,4,2,128]{0,3,1,2:T(8,128)(2,1)} %bitcast.34) | data formatting | bytes 14155776 | tf_op jit(solution)/shard_map/cthkw,cthiw->ki/dot_general | solution.py:55
  38.0 1.3 all-gather.4.cloned.1.call-done
  39.2 6.6 %fusion.15 = f32[3,3,3,128,512,1,1]{4,3,2,1,0,6,5:T(8,128)S(1)} fusion(bf16[3,3,3,128,4,2,128]{6,3,2,1,0,5,4:T(8,128)(2,1)} %bitcast.35, bf16[1,2,4,512,128]{4,3,2,1,0:T(8,128)(2,1)} %all-gather.4.cloned.1.call-done), kind=kOutput, calls=%fused_computation.20 | convolution fusion | flops 3627024384 | bytes 15204352 | tf_op jit(solution)/shard_map/cthkw,cthiw->ki/dot_general | solution.py:55
  45.9 3.7 %copy.47 = f32[3,3,3,128,512,1,1]{4,3,0,1,2,5,6:T(8,128)} copy(f32[3,3,3,128,512,1,1]{4,3,2,1,0,6,5:T(8,128)S(1)} %fusion.15) | data formatting | bytes 14155776 | tf_op jit(solution)/shard_map/cthkw,cthiw->ki/dot_general | solution.py:55
  49.7 7.6 %fusion.11 = f32[1,2,4,512,128]{3,4,2,1,0:T(8,128)} fusion(bf16[3456,512,1,1]{1,0,3,2:T(8,128)(2,1)S(1)} %bitcast.31, bf16[1,2,4,3456,128]{3,4,2,1,0:T(8,128)(2,1)} %copy-done.2), kind=kOutput, calls=%fused_computation.18 | convolution fusion | flops 3623878656 | bytes 12713984 | tf_op jit(solution)/shard_map/cthkw,ki->cthiw/dot_general | solution.py:63
  57.3 7.9 %reduce-scatter.5.cloned.1.call-done = f32[3,3,3,64,512]{4,3,0,1,2:T(8,128)} async-done(((f32[3,3,3,128,512]{4,3,0,1,2:T(8,128)}), f32[3,3,3,64,512]{4,3,0,1,2:T(8,128)}) %reduce-scatter.5.cloned.1.call-update) | async-done | bytes 3538960 | tf_op jit(solution)/shard_map/reduce_scatter | solution.py:59
  65.2 4.4 %copy.36 = f32[3,3,3,64,512]{4,3,2,1,0:T(8,128)} copy(f32[3,3,3,64,512]{4,3,0,1,2:T(8,128)} %reduce-scatter.5.cloned.1.call-done) | data formatting | bytes 7077888 | tf_op jit(solution)/shard_map/reduce_scatter | solution.py:59
  69.6 1.8 copy.32
  71.4 33.5 %reduce-scatter.3.cloned.1.call-done = f32[1,2,4,128,128]{3,4,2,1,0:T(8,128)} async-done(((f32[1,2,4,512,128]{3,4,2,1,0:T(8,128)}), f32[1,2,4,128,128]{3,4,2,1,0:T(8,128)}) %reduce-scatter.3.cloned.1.call-update) | async-done | bytes 524304 | tf_op jit(solution)/shard_map/reduce_scatter | solution.py:66
  104.9 2.0 fusion.28
  106.9 1.8 copy.37
  108.7 242.1 %all-gather.6.cloned.1.call-done = f32[12,3,3,64,512]{4,3,2,1,0:T(8,128)} async-done(((f32[3,3,3,64,512]{4,3,2,1,0:T(8,128)}), f32[12,3,3,64,512]{4,3,2,1,0:T(8,128)}) %all-gather.6.cloned.1.call-update) | async-done | bytes 14155792 | tf_op jit(solution)/shard_map/all_gather | solution.py:60
  350.8 9.0 %reduce_sum.9 = f32[3,3,3,64,512]{4,3,2,1,0:T(8,128)} reduce(f32[4,3,3,3,64,512]{5,4,3,2,1,0:T(8,128)} %bitcast.33, f32[]{:T(128)} %constant.3.clone.1), dimensions={0}, to_apply=%region_2.3 | reduce | flops 2654208 | bytes 17694724 | tf_op jit(solution)/shard_map/reduce_sum | solution.py:60
  359.9 4.4 %broadcast_multiply_fusion = f32[3,3,3,64,512]{4,3,2,1,0:T(8,128)} fusion(f32[3,3,3,64,512]{4,3,2,1,0:T(8,128)} %reduce_sum.9), kind=kLoop, calls=%fused_computation.11 | loop fusion | flops 884736 | bytes 7077888 | tf_op jit(solution)/shard_map/mul | solution.py:61
  (38 shorter events, 2.4 us)
Async XLA Ops:
  7.2 42.5 %copy-start = (bf16[3,3,3,128,512]{4,3,2,1,0:T(8,128)(2,1)S(1)}, bf16[3,3,3,128,512]{4,3,2,1,0:T(8,128)(2,1)}, u32[]{:S(2)}) copy-start(bf16[3,3,3,128,512]{4,3,2,1,0:T(8,128)(2,1)} %param.5) | copy-start | bytes 10616836
  7.2 32.0 %all-gather.4.cloned.1.call-start = ((), (), s32[]{:S(2)}) async-start(), calls=%async_computation.3 | async-start | bytes 1310720 | tf_op jit(solution)/shard_map/all_gather | solution.py:49
  7.9 57.3 %reduce-scatter.5.cloned.1.call-start = ((), (), s32[]{:S(2)}) async-start(), calls=%async_computation.4 | async-start | bytes 10616832 | tf_op jit(solution)/shard_map/reduce_scatter | solution.py:59
  10.0 14.2 %copy-start.1 = (bf16[1,2,4,128,128]{3,4,2,1,0:T(8,128)(2,1)S(1)}, bf16[1,2,4,128,128]{3,4,2,1,0:T(8,128)(2,1)}, u32[]{:S(2)}) copy-start(bf16[1,2,4,128,128]{3,4,2,1,0:T(8,128)(2,1)} %copy.26) | copy-start | bytes 786436
  11.0 7.1 %collective-permute-start = (bf16[1,2,1,128,128]{3,4,2,1,0:T(8,128)(2,1)S(1)}, bf16[1,2,1,128,128]{3,4,2,1,0:T(8,128)(2,1)S(1)}, u32[]{:S(2)}, u32[]{:S(2)}) collective-permute-start(bf16[1,2,1,128,128]{3,4,2,1,0:T(8,128)(2,1)S(1)} %get-tuple-element.8), channel_id=1, source_target_pairs={{0,2},{2,4},{4,6},{1,3},{3,5},{5,7},{8,10},{10,12},{12,14},{9,11},... | collective-permute-start | bytes 196616 | tf_op jit(solution)/shard_map/ppermute | solution.py:15
  15.9 6.2 %collective-permute-start.1 = (bf16[1,2,1,128,128]{3,4,2,1,0:T(8,128)(2,1)S(1)}, bf16[1,2,1,128,128]{3,4,2,1,0:T(8,128)(2,1)S(1)}, u32[]{:S(2)}, u32[]{:S(2)}) collective-permute-start(bf16[1,2,1,128,128]{3,4,2,1,0:T(8,128)(2,1)S(1)} %get-tuple-element.9), channel_id=1, source_target_pairs={{2,0},{4,2},{6,4},{3,1},{5,3},{7,5},{10,8},{12,10},{14,12},{11,9},... | collective-permute-start | bytes 196616 | tf_op jit(solution)/shard_map/ppermute | solution.py:17
  25.0 2.9 copy-start.2
  49.6 55.3 %reduce-scatter.3.cloned.1.call-start = ((), (), s32[]{:S(2)}) async-start(), calls=%async_computation.2 | async-start | bytes 2621440 | tf_op jit(solution)/shard_map/reduce_scatter | solution.py:66
  57.3 293.6 %all-gather.6.cloned.1.call-start = ((), (), s32[]{:S(2)}) async-start(), calls=%async_computation.5 | async-start | bytes 17694720 | tf_op jit(solution)/shard_map/all_gather | solution.py:60
Sparse Core Ops, SparseCore 0:
  9.9 29.3 all-gather.3
  49.8 15.4 reduce-scatter.4
  68.5 36.3 reduce-scatter.2
  106.9 243.9 all-gather.5
